TPU v7x, 32 devices: a whole 2x2x4 slice. The times are simulated.
32 devices in a mesh: dp: 8 (over z, x), tensor: 4 (over y, core).
Axes of the slice: x: 2, y: 2, z: 4, core: 2. Of those that a mesh axis runs over, the one named last changes fastest.
Arguments:
- tokens: bfloat16 [16384, 1024], P(('dp', 'tensor')), may hold values from -6 to 6
- doc_ids: int32 [16, 1024], P('dp'), may hold values from 0 to 7, never falling along the last dimension, each value on 1 to 800 neighbouring positions
- mixer_norm: bfloat16 [1024], P('dp'), may hold values from 0.25 to 1.75
- in_weight: bfloat16 [1024, 3, 1024], P('dp', None, 'tensor'), may hold values from -0.1875 to 0.1875
- conv_weight: bfloat16 [3, 1024], P(None, 'dp'), may hold values from -3.5 to 3.5
- out_weight: bfloat16 [1024, 1024], P('tensor', 'dp'), may hold values from -0.1875 to 0.1875
- feed_norm: bfloat16 [1024], P('dp'), may hold values from 0.25 to 1.75
- gate_weight: bfloat16 [1024, 4608], P('dp', 'tensor'), may hold values from -0.1875 to 0.1875
- up_weight: bfloat16 [1024, 4608], P('dp', 'tensor'), may hold values from -0.1875 to 0.1875
- down_weight: bfloat16 [4608, 1024], P('tensor', 'dp'), may hold values from -0.09375 to 0.09375
- out_grad: bfloat16 [16384, 1024], P(('dp', 'tensor')), may hold values from -6 to 6
Outputs:
- output: bfloat16 [16384, 1024], P(('dp', 'tensor'))
- input_grad: bfloat16 [16384, 1024], P(('dp', 'tensor'))
- mixer_norm_grad: float32 [1024], P('dp')
- in_weight_grad: float32 [1024, 3, 1024], P('dp', None, 'tensor')
- conv_weight_grad: float32 [3, 1024], P(None, 'dp')
- out_weight_grad: float32 [1024, 1024], P('tensor', 'dp')
- feed_norm_grad: float32 [1024], P('dp')
- gate_weight_grad: float32 [1024, 4608], P('dp', 'tensor')
- up_weight_grad: float32 [1024, 4608], P('dp', 'tensor')
- down_weight_grad: float32 [4608, 1024], P('tensor', 'dp')
Inputs may be any that keep to these rules, and one draw needn't show every extreme that they name: `doc_ids`: within each sequence the document numbers never fall; a document covers 1 to 800 consecutive tokens and one covers exactly 800.
All inputs are finite; a program needn't handle non-finite values.
Results may differ from a plain program's by a relative error of at most 0.015.
Values may be sent and summed in bfloat16 or wider, within the bound.
A program may use at most 128 MiB of HBM per device.

v0:
```python
import jax
import jax.numpy as jnp
from jax import lax
from jax.sharding import PartitionSpec as P

KW = 3


epsilon = 1e-05


def shift_down(values, offset):
    if offset == 0:
        return values
    padding = jnp.zeros((offset,) + values.shape[1:], values.dtype)
    return jnp.concatenate([padding, values[:-offset]], axis=0)


def shift_up(values, offset):
    if offset == 0:
        return values
    padding = jnp.zeros((offset,) + values.shape[1:], values.dtype)
    return jnp.concatenate([values[offset:], padding], axis=0)


def tap_masks(doc_rows):
    total_rows = doc_rows.shape[0] * doc_rows.shape[1]
    tap_keep = [jnp.ones((total_rows,), jnp.float32)]
    for offset in range(1, KW):
        matching = doc_rows[:, offset:] == doc_rows[:, :-offset]
        leading = jnp.zeros((doc_rows.shape[0], offset), dtype=bool)
        matching = jnp.concatenate([leading, matching], axis=1)
        tap_keep.append(jnp.where(matching, 1.0, 0.0).astype(jnp.float32).reshape(total_rows))
    return jnp.stack(tap_keep)


def norm_back(grad_out, unit_rows, inverse, gain):
    scaled = grad_out * gain
    return inverse * (scaled - unit_rows * jnp.mean(scaled * unit_rows, axis=-1, keepdims=True))


def body(
    tokens,
    doc_ids,
    mixer_norm,
    in_weight,
    conv_weight,
    out_weight,
    feed_norm,
    gate_weight,
    up_weight,
    down_weight,
    out_grad,
):
    model_width = tokens.shape[1]
    gathered = (
        lax.all_gather(mixer_norm, "dp", axis=0, tiled=True),
        lax.all_gather(in_weight, "dp", axis=0, tiled=True),
        lax.all_gather(conv_weight, "dp", axis=1, tiled=True),
        lax.all_gather(out_weight, "dp", axis=1, tiled=True),
        lax.all_gather(feed_norm, "dp", axis=0, tiled=True),
        lax.all_gather(gate_weight, "dp", axis=0, tiled=True),
        lax.all_gather(up_weight, "dp", axis=0, tiled=True),
        lax.all_gather(down_weight, "dp", axis=1, tiled=True),
    )
    norm_one, in_full, conv_full, out_full, norm_two, gate_full, up_full, down_full = gathered
    channels = in_full.shape[2]
    channel_start = lax.axis_index("tensor") * channels
    tap_keep = tap_masks(doc_ids)
    conv_taps = lax.dynamic_slice_in_dim(conv_full, channel_start, channels, 1).astype(jnp.float32)
    inputs = tokens.astype(jnp.float32)
    inverse_one = lax.rsqrt(jnp.mean(inputs * inputs, axis=-1, keepdims=True) + epsilon)
    unit_one = inputs * inverse_one
    normed_local = (unit_one * norm_one.astype(jnp.float32)).astype(jnp.bfloat16)
    normed = lax.all_gather(normed_local, "tensor", axis=0, tiled=True)
    projected = jnp.einsum("td,dkc->tkc", normed, in_full, preferred_element_type=jnp.float32)
    input_gate = projected[:, 0]
    output_gate = projected[:, 1]
    values = projected[:, 2]
    mixed_input = input_gate * values
    convolved = sum(
        (
            tap_keep[offset][:, None] * conv_taps[offset][None, :] * shift_down(mixed_input, offset)
            for offset in range(KW)
        )
    )
    mixer_in = (output_gate * convolved).astype(jnp.bfloat16)
    mixer_out = lax.psum_scatter(
        jnp.dot(mixer_in, out_full, preferred_element_type=jnp.float32),
        "tensor",
        scatter_dimension=0,
        tiled=True,
    )
    hidden = inputs + mixer_out
    inverse_two = lax.rsqrt(jnp.mean(hidden * hidden, axis=-1, keepdims=True) + epsilon)
    unit_two = hidden * inverse_two
    normed_two_local = (unit_two * norm_two.astype(jnp.float32)).astype(jnp.bfloat16)
    normed_two = lax.all_gather(normed_two_local, "tensor", axis=0, tiled=True)
    gate_pre = jnp.dot(normed_two, gate_full, preferred_element_type=jnp.float32)
    upward = jnp.dot(normed_two, up_full, preferred_element_type=jnp.float32)
    activated = (jax.nn.silu(gate_pre) * upward).astype(jnp.bfloat16)
    feed_out = lax.psum_scatter(
        jnp.dot(activated, down_full, preferred_element_type=jnp.float32).astype(jnp.bfloat16),
        "tensor",
        scatter_dimension=0,
        tiled=True,
    ).astype(jnp.float32)
    output = (hidden + feed_out).astype(jnp.bfloat16)
    regathered = (
        lax.all_gather(mixer_norm, "dp", axis=0, tiled=True),
        lax.all_gather(in_weight, "dp", axis=0, tiled=True),
        lax.all_gather(conv_weight, "dp", axis=1, tiled=True),
        lax.all_gather(out_weight, "dp", axis=1, tiled=True),
        lax.all_gather(feed_norm, "dp", axis=0, tiled=True),
        lax.all_gather(gate_weight, "dp", axis=0, tiled=True),
        lax.all_gather(up_weight, "dp", axis=0, tiled=True),
        lax.all_gather(down_weight, "dp", axis=1, tiled=True),
    )
    norm_one_b, in_again, conv_again, out_again, norm_two_b, gate_again, up_again, down_again = (
        regathered
    )
    gain_one = norm_one_b.astype(jnp.float32)
    gain_two = norm_two_b.astype(jnp.float32)
    taps_again = lax.dynamic_slice_in_dim(conv_again, channel_start, channels, 1).astype(
        jnp.float32
    )
    sigmoid = jax.nn.sigmoid(gate_pre)
    cotangent = lax.all_gather(out_grad, "tensor", axis=0, tiled=True)
    down_grad = jnp.einsum("tf,td->fd", activated, cotangent, preferred_element_type=jnp.float32)
    grad_act = jnp.einsum("td,fd->tf", cotangent, down_again, preferred_element_type=jnp.float32)
    grad_gate = (grad_act * upward * sigmoid * (1.0 + gate_pre * (1.0 - sigmoid))).astype(
        jnp.bfloat16
    )
    grad_up = (grad_act * gate_pre * sigmoid).astype(jnp.bfloat16)
    gate_grad = jnp.einsum("td,tf->df", normed_two, grad_gate, preferred_element_type=jnp.float32)
    up_grad = jnp.einsum("td,tf->df", normed_two, grad_up, preferred_element_type=jnp.float32)
    grad_two = lax.psum_scatter(
        (
            jnp.einsum("tf,df->td", grad_gate, gate_again, preferred_element_type=jnp.float32)
            + jnp.einsum("tf,df->td", grad_up, up_again, preferred_element_type=jnp.float32)
        ).astype(jnp.bfloat16),
        "tensor",
        scatter_dimension=0,
        tiled=True,
    ).astype(jnp.float32)
    feed_gain_part = jnp.sum(grad_two * unit_two, axis=0)
    grad_hidden = out_grad.astype(jnp.float32) + norm_back(
        grad_two, unit_two, inverse_two, gain_two
    )
    grad_mix_local = grad_hidden.astype(jnp.bfloat16)
    grad_mix = lax.all_gather(grad_mix_local, "tensor", axis=0, tiled=True)
    out_grad_part = jnp.einsum("tc,td->cd", mixer_in, grad_mix, preferred_element_type=jnp.float32)
    grad_in = jnp.einsum("td,cd->tc", grad_mix, out_again, preferred_element_type=jnp.float32)
    grad_c = grad_in * convolved
    grad_conv = grad_in * output_gate
    grad_mixed = sum(
        (
            taps_again[offset][None, :] * shift_up(tap_keep[offset][:, None] * grad_conv, offset)
            for offset in range(KW)
        )
    )
    tap_grad = jnp.stack(
        [
            jnp.sum(tap_keep[offset][:, None] * grad_conv * shift_down(mixed_input, offset), axis=0)
            for offset in range(KW)
        ]
    )
    grad_projected = jnp.stack(
        [grad_mixed * values, grad_c, grad_mixed * input_gate], axis=1
    ).astype(jnp.bfloat16)
    in_grad_part = jnp.einsum(
        "td,tkc->dkc", normed, grad_projected, preferred_element_type=jnp.float32
    )
    grad_one = lax.psum_scatter(
        jnp.einsum(
            "tkc,dkc->td", grad_projected, in_again, preferred_element_type=jnp.float32
        ).astype(jnp.bfloat16),
        "tensor",
        scatter_dimension=0,
        tiled=True,
    ).astype(jnp.float32)
    mixer_gain_part = jnp.sum(grad_one * unit_one, axis=0)
    input_grad = (grad_hidden + norm_back(grad_one, unit_one, inverse_one, gain_one)).astype(
        jnp.bfloat16
    )
    conv_part = lax.dynamic_update_slice_in_dim(
        jnp.zeros((KW, model_width), jnp.float32), tap_grad, channel_start, 1
    )
    summed = (
        lax.psum_scatter(mixer_gain_part, "dp", scatter_dimension=0, tiled=True),
        lax.psum_scatter(in_grad_part, "dp", scatter_dimension=0, tiled=True),
        lax.psum_scatter(conv_part, "dp", scatter_dimension=1, tiled=True),
        lax.psum_scatter(out_grad_part, "dp", scatter_dimension=1, tiled=True),
        lax.psum_scatter(feed_gain_part, "dp", scatter_dimension=0, tiled=True),
        lax.psum_scatter(gate_grad, "dp", scatter_dimension=0, tiled=True),
        lax.psum_scatter(up_grad, "dp", scatter_dimension=0, tiled=True),
        lax.psum_scatter(down_grad, "dp", scatter_dimension=1, tiled=True),
    )
    (
        mixer_gain_sum,
        in_weight_grad,
        conv_sum,
        out_weight_grad,
        feed_gain_sum,
        gate_weight_grad,
        up_weight_grad,
        down_weight_grad,
    ) = summed
    mixer_norm_grad, conv_weight_grad, feed_norm_grad = lax.psum(
        (mixer_gain_sum, conv_sum, feed_gain_sum), "tensor"
    )
    return (
        output,
        input_grad,
        mixer_norm_grad,
        in_weight_grad,
        conv_weight_grad,
        out_weight_grad,
        feed_norm_grad,
        gate_weight_grad,
        up_weight_grad,
        down_weight_grad,
    )


def solution(mesh):
    in_specs = (
        P(("dp", "tensor"), None),
        P("dp", None),
        P("dp"),
        P("dp", None, "tensor"),
        P(None, "dp"),
        P("tensor", "dp"),
        P("dp"),
        P("dp", "tensor"),
        P("dp", "tensor"),
        P("tensor", "dp"),
        P(("dp", "tensor"), None),
    )
    out_specs = (
        P(("dp", "tensor"), None),
        P(("dp", "tensor"), None),
        P("dp"),
        P("dp", None, "tensor"),
        P(None, "dp"),
        P("tensor", "dp"),
        P("dp"),
        P("dp", "tensor"),
        P("dp", "tensor"),
        P("tensor", "dp"),
    )
    return jax.shard_map(body, mesh=mesh, in_specs=in_specs, out_specs=out_specs, check_vma=False)
```

profile of v0, /device:TPU:0, one launch (start us, length us, event | category | flops | bytes accessed | tf_op | source)
XLA Modules:
  0.0 1157.0 jit_solution(12450127459325141186)
XLA Ops:
  8.0 22.3 %all-gather = bf16[8,1,128]{2,1,0:T(2,128)(2,1)S(1)} all-gather(bf16[1,1,128]{2,1,0:T(2,128)(2,1)} %bitcast.112), channel_id=1, replica_groups=mesh['dp'=8,'tensor'=4] {'dp'}, dimensions={0}, use_global_device_ids=true | all-gather | bytes 2304 | tf_op jit(solution)/shard_map/all_gather | solution.py:57
  34.5 16.3 %all_gather.47 = bf16[3,1024]{1,0:T(4,128)(2,1)S(1)} all-gather(bf16[3,128]{1,0:T(4,128)(2,1)S(1)} %copy-done.17), channel_id=1, replica_groups=mesh['dp'=8,'tensor'=4] {'dp'}, dimensions={1}, use_global_device_ids=true | all-gather | bytes 6912 | tf_op jit(solution)/shard_map/all_gather | solution.py:59
  51.2 30.1 %all_gather.48 = bf16[256,1024]{1,0:T(8,128)(2,1)} all-gather(bf16[256,128]{1,0:T(8,128)(2,1)S(1)} %copy-done.14), channel_id=1, replica_groups=mesh['dp'=8,'tensor'=4] {'dp'}, dimensions={1}, use_global_device_ids=true | all-gather | bytes 589824 | tf_op jit(solution)/shard_map/all_gather | solution.py:60
  81.3 15.1 %all-gather.11.cloned.1.call-done = bf16[2048,1024]{1,0:T(8,128)(2,1)} async-done(((bf16[512,1024]{1,0:T(8,128)(2,1)}), bf16[2048,1024]{1,0:T(8,128)(2,1)}) %all-gather.11.cloned.1.call-update) | async-done | bytes 4194320 | tf_op jit(solution)/shard_map/all_gather | solution.py:75
  112.1 20.4 %all-gather.1 = bf16[8,1,128]{2,1,0:T(2,128)(2,1)S(1)} all-gather(bf16[1,1,128]{2,1,0:T(2,128)(2,1)S(1)} %bitcast.113), channel_id=1, replica_groups=mesh['dp'=8,'tensor'=4] {'dp'}, dimensions={0}, use_global_device_ids=true | all-gather | bytes 2304 | tf_op jit(solution)/shard_map/all_gather | solution.py:61
  132.5 50.9 %reduce-scatter.13.cloned.1.call-done = f32[512,1024]{1,0:T(8,128)} async-done(((f32[2048,1024]{1,0:T(8,128)}), f32[512,1024]{1,0:T(8,128)}) %reduce-scatter.13.cloned.1.call-update) | async-done | bytes 2097168 | tf_op jit(solution)/shard_map/reduce_scatter | solution.py:88
  190.1 47.6 %all-gather.17.cloned.1.call-done = bf16[1024,1152]{1,0:T(8,128)(2,1)} async-done(((bf16[128,1152]{1,0:T(8,128)(2,1)}), bf16[1024,1152]{1,0:T(8,128)(2,1)}) %all-gather.17.cloned.1.call-update) | async-done | bytes 2359312 | tf_op jit(solution)/shard_map/all_gather | solution.py:62
  237.7 35.1 %all-gather.15.cloned.1.call-done = bf16[2048,1024]{1,0:T(8,128)(2,1)} async-done(((bf16[512,1024]{1,0:T(8,128)(2,1)}), bf16[2048,1024]{1,0:T(8,128)(2,1)}) %all-gather.15.cloned.1.call-update) | async-done | bytes 4194320 | tf_op jit(solution)/shard_map/all_gather | solution.py:98
  283.1 44.1 %all-gather.19.cloned.1.call-done = bf16[1024,1152]{1,0:T(8,128)(2,1)} async-done(((bf16[128,1152]{1,0:T(8,128)(2,1)}), bf16[1024,1152]{1,0:T(8,128)(2,1)}) %all-gather.19.cloned.1.call-update) | async-done | bytes 2359312 | tf_op jit(solution)/shard_map/all_gather | solution.py:63
  337.4 44.4 %all-gather.21.cloned.1.call-done = bf16[1152,1024]{1,0:T(8,128)(2,1)} async-done(((bf16[1152,128]{1,0:T(8,128)(2,1)}), bf16[1152,1024]{1,0:T(8,128)(2,1)}) %all-gather.21.cloned.1.call-update) | async-done | bytes 2359312 | tf_op jit(solution)/shard_map/all_gather | solution.py:64
  381.8 34.3 %all-gather.23.cloned.1.call-done = bf16[2048,1024]{1,0:T(8,128)(2,1)} async-done(((bf16[512,1024]{1,0:T(8,128)(2,1)}), bf16[2048,1024]{1,0:T(8,128)(2,1)}) %all-gather.23.cloned.1.call-update) | async-done | bytes 4194320 | tf_op jit(solution)/shard_map/all_gather | solution.py:128
  416.1 18.0 %multiply_convert_fusion = (bf16[2048,1152]{1,0:T(8,128)(2,1)}, bf16[2048,1152]{1,0:T(8,128)(2,1)}, bf16[2048,1152]{1,0:T(8,128)(2,1)}) fusion(f32[2048,1152]{1,0:T(8,128)} %fusion.35, f32[2048,1152]{1,0:T(8,128)} %fusion.36, bf16[2048,1024]{1,0:T(8,128)(2,1)} %all-gather.23.cloned.1.call-done, bf16[1152,1024]{1,0:T(8,128)(2,1)} %all-gather.21.cloned.1.call-done), kind=kOutput, calls=%fused_computation | convolution fusion | flops 4869586944 | bytes 39583744 | tf_op jit(solution)/shard_map/td,fd->tf/dot_general | solution.py:130
  449.7 44.6 %reduce-scatter.17.cloned.1.call-done = bf16[512,1024]{1,0:T(8,128)(2,1)} async-done(((bf16[2048,1024]{1,0:T(8,128)(2,1)}), bf16[512,1024]{1,0:T(8,128)(2,1)}) %reduce-scatter.17.cloned.1.call-update) | async-done | bytes 1048592 | tf_op jit(solution)/shard_map/reduce_scatter | solution.py:137
  500.1 34.6 %all-gather.25.cloned.1.call-done = bf16[2048,1024]{1,0:T(8,128)(2,1)} async-done(((bf16[512,1024]{1,0:T(8,128)(2,1)}), bf16[2048,1024]{1,0:T(8,128)(2,1)}) %all-gather.25.cloned.1.call-update) | async-done | bytes 4194320 | tf_op jit(solution)/shard_map/all_gather | solution.py:151
  566.2 10.4 fusion.39
  576.7 10.4 fusion.40
  613.6 43.5 %reduce-scatter.19.cloned.1.call-done = bf16[512,1024]{1,0:T(8,128)(2,1)} async-done(((bf16[2048,1024]{1,0:T(8,128)(2,1)}), bf16[512,1024]{1,0:T(8,128)(2,1)}) %reduce-scatter.19.cloned.1.call-update) | async-done | bytes 1048592 | tf_op jit(solution)/shard_map/reduce_scatter | solution.py:174
  659.1 21.6 %all-reduce.8 = (f32[1024]{0:T(1024)S(1)}, f32[1024]{0:T(1024)S(1)}) all-reduce(f32[1024]{0:T(1024)S(1)} %get-tuple-element.12, f32[1024]{0:T(1024)S(1)} %get-tuple-element.10), channel_id=6, replica_groups=mesh['dp'=8,'tensor'=4] {'dp'}, use_global_device_ids=true, to_apply=%region_9.10.clone | all-reduce | flops 2048 | bytes 16384
  687.6 16.7 %reduce-scatter.15.cloned.1.call-done = bf16[512,1024]{1,0:T(8,128)(2,1)} async-done(((bf16[2048,1024]{1,0:T(8,128)(2,1)}), bf16[512,1024]{1,0:T(8,128)(2,1)}) %reduce-scatter.15.cloned.1.call-update) | async-done | bytes 1048592 | tf_op jit(solution)/shard_map/reduce_scatter | solution.py:102
  708.2 96.1 %reduce-scatter.25.cloned.1.call-done = f32[128,1152]{1,0:T(8,128)} async-done(((f32[1024,1152]{1,0:T(8,128)}), f32[128,1152]{1,0:T(8,128)}) %reduce-scatter.25.cloned.1.call-update) | async-done | bytes 589840 | tf_op jit(solution)/shard_map/reduce_scatter | solution.py:195
  804.3 99.7 %reduce-scatter.27.cloned.1.call-done = f32[128,1152]{1,0:T(8,128)} async-done(((f32[1024,1152]{1,0:T(8,128)}), f32[128,1152]{1,0:T(8,128)}) %reduce-scatter.27.cloned.1.call-update) | async-done | bytes 589840 | tf_op jit(solution)/shard_map/reduce_scatter | solution.py:196
  904.0 100.1 %reduce-scatter.29.cloned.1.call-done = f32[1152,128]{1,0:T(8,128)} async-done(((f32[1152,1024]{1,0:T(8,128)}), f32[1152,128]{1,0:T(8,128)}) %reduce-scatter.29.cloned.1.call-update) | async-done | bytes 589840 | tf_op jit(solution)/shard_map/reduce_scatter | solution.py:197
  1004.1 67.8 %reduce-scatter.23.cloned.1.call-done = f32[256,128]{1,0:T(8,128)} async-done(((f32[256,1024]{1,0:T(8,128)}), f32[256,128]{1,0:T(8,128)}) %reduce-scatter.23.cloned.1.call-update) | async-done | bytes 131088 | tf_op jit(solution)/shard_map/reduce_scatter | solution.py:193
  1071.9 78.0 %reduce-scatter.21.cloned.1.call-done = f32[128,3,256]{2,0,1:T(8,128)} async-done(((f32[1024,3,256]{2,0,1:T(8,128)}), f32[128,3,256]{2,0,1:T(8,128)}) %reduce-scatter.21.cloned.1.call-update) | async-done | bytes 393232 | tf_op jit(solution)/shard_map/reduce_scatter | solution.py:191
  (132 shorter events, 139.5 us)
Async XLA Ops:
  7.2 44.0 %copy-start.14 = (bf16[256,128]{1,0:T(8,128)(2,1)S(1)}, bf16[256,128]{1,0:T(8,128)(2,1)}, u32[]{:S(2)}) copy-start(bf16[256,128]{1,0:T(8,128)(2,1)} %param.16) | copy-start | bytes 196612
  7.2 74.0 %all-gather.13.cloned.1.call-start = ((), (), s32[]{:S(2)}) async-start(), calls=%async_computation.11 | async-start | bytes 1769472 | tf_op jit(solution)/shard_map/all_gather | solution.py:58
  7.9 88.4 %all-gather.11.cloned.1.call-start = ((), (), s32[]{:S(2)}) async-start(), calls=%async_computation.10 | async-start | bytes 5242880 | tf_op jit(solution)/shard_map/all_gather | solution.py:75
  30.3 50.9 %copy-start.12 = (f32[8,1,128]{2,1,0:T(1,128)}, f32[8,1,128]{2,1,0:T(1,128)S(1)}, u32[]{:S(2)}) copy-start(f32[8,1,128]{2,1,0:T(1,128)S(1)} %convert_element_type.84) | copy-start | bytes 12292
  34.4 149.0 %reduce-scatter.13.cloned.1.call-start = ((), (), s32[]{:S(2)}) async-start(), calls=%async_computation.12 | async-start | bytes 10485760 | tf_op jit(solution)/shard_map/reduce_scatter | solution.py:88
  111.4 71.9 %copy-start.4 = (bf16[512,1024]{1,0:T(8,128)(2,1)S(1)}, bf16[512,1024]{1,0:T(8,128)(2,1)}, u32[]{:S(2)}) copy-start(bf16[512,1024]{1,0:T(8,128)(2,1)} %param.11) | copy-start | bytes 3145732
  111.5 126.3 %all-gather.17.cloned.1.call-start = ((), (), s32[]{:S(2)}) async-start(), calls=%async_computation.14 | async-start | bytes 2654208 | tf_op jit(solution)/shard_map/all_gather | solution.py:62
  112.1 160.8 %all-gather.15.cloned.1.call-start = ((), (), s32[]{:S(2)}) async-start(), calls=%async_computation.13 | async-start | bytes 5242880 | tf_op jit(solution)/shard_map/all_gather | solution.py:98
  187.8 139.4 %all-gather.19.cloned.1.call-start = ((), (), s32[]{:S(2)}) async-start(), calls=%async_computation.15 | async-start | bytes 2654208 | tf_op jit(solution)/shard_map/all_gather | solution.py:63
  188.4 193.4 %all-gather.21.cloned.1.call-start = ((), (), s32[]{:S(2)}) async-start(), calls=%async_computation.16 | async-start | bytes 2654208 | tf_op jit(solution)/shard_map/all_gather | solution.py:64
  189.2 227.0 %all-gather.23.cloned.1.call-start = ((), (), s32[]{:S(2)}) async-start(), calls=%async_computation.18 | async-start | bytes 5242880 | tf_op jit(solution)/shard_map/all_gather | solution.py:128
  189.9 304.5 %reduce-scatter.17.cloned.1.call-start = ((), (), s32[]{:S(2)}) async-start(), calls=%async_computation.19 | async-start | bytes 5242880 | tf_op jit(solution)/shard_map/reduce_scatter | solution.py:137
  449.7 85.0 %all-gather.25.cloned.1.call-start = ((), (), s32[]{:S(2)}) async-start(), calls=%async_computation.20 | async-start | bytes 5242880 | tf_op jit(solution)/shard_map/all_gather | solution.py:151
  500.1 112.6 %reduce-scatter.31.cloned.1.call-start = ((), (), s32[]{:S(2)}) async-start(), calls=%async_computation.27 | async-start | bytes 589824
  548.9 108.2 %reduce-scatter.19.cloned.1.call-start = ((), (), s32[]{:S(2)}) async-start(), calls=%async_computation.21 | async-start | bytes 5242880 | tf_op jit(solution)/shard_map/reduce_scatter | solution.py:174
  556.2 148.1 %reduce-scatter.15.cloned.1.call-start = ((), (), s32[]{:S(2)}) async-start(), calls=%async_computation.17 | async-start | bytes 5242880 | tf_op jit(solution)/shard_map/reduce_scatter | solution.py:102
  566.2 238.1 %reduce-scatter.25.cloned.1.call-start = ((), (), s32[]{:S(2)}) async-start(), calls=%async_computation.24 | async-start | bytes 5308416 | tf_op jit(solution)/shard_map/reduce_scatter | solution.py:195
  576.6 327.4 %reduce-scatter.27.cloned.1.call-start = ((), (), s32[]{:S(2)}) async-start(), calls=%async_computation.25 | async-start | bytes 5308416 | tf_op jit(solution)/shard_map/reduce_scatter | solution.py:196
  587.1 417.1 %reduce-scatter.29.cloned.1.call-start = ((), (), s32[]{:S(2)}) async-start(), calls=%async_computation.26 | async-start | bytes 5308416 | tf_op jit(solution)/shard_map/reduce_scatter | solution.py:197
  596.9 475.0 %reduce-scatter.23.cloned.1.call-start = ((), (), s32[]{:S(2)}) async-start(), calls=%async_computation.23 | async-start | bytes 1179648 | tf_op jit(solution)/shard_map/reduce_scatter | solution.py:193
  602.6 547.3 %reduce-scatter.21.cloned.1.call-start = ((), (), s32[]{:S(2)}) async-start(), calls=%async_computation.22 | async-start | bytes 3538944 | tf_op jit(solution)/shard_map/reduce_scatter | solution.py:191
  610.8 46.3 %copy-start.13 = (f32[8,1,128]{2,1,0:T(1,128)S(1)}, f32[8,1,128]{2,1,0:T(1,128)}, u32[]{:S(2)}) copy-start(f32[8,1,128]{2,1,0:T(1,128)} %copy-done.12) | copy-start | bytes 12292
  610.8 46.3 %copy-start.16 = (f32[512]{0:T(512)S(1)}, f32[512]{0:T(512)}, u32[]{:S(2)}) copy-start(f32[512]{0:T(512)} %copy-done.15) | copy-start | bytes 6148
  610.8 93.5 %copy-start.3 = (f32[512,1024]{1,0:T(8,128)S(1)}, f32[512,1024]{1,0:T(8,128)}, u32[]{:S(2)}) copy-start(f32[512,1024]{1,0:T(8,128)} %copy-done.1) | copy-start | bytes 6291460
  (17 other events, 150.9 us)
Sparse Core Ops, SparseCore 0:
  10.2 47.3 all-gather.12
  59.7 36.5 all-gather.10
  111.6 71.7 reduce-scatter.12
  185.6 52.0 all-gather.16
  239.8 33.0 all-gather.14
  275.1 52.0 all-gather.18
  329.5 52.2 all-gather.20
  383.4 32.6 all-gather.22
  449.8 44.5 reduce-scatter.16
  500.2 34.4 all-gather.24
  549.1 61.9 reduce-scatter.30
  613.5 43.5 reduce-scatter.18
  659.6 44.6 reduce-scatter.14
  708.8 95.4 reduce-scatter.24
  808.8 95.1 reduce-scatter.26
  908.6 95.5 reduce-scatter.28
  1008.3 63.5 reduce-scatter.22
  1076.0 73.9 reduce-scatter.20
where the time goes:
time: 1160 us
  waiting for transfers between devices  856 us (74%)
  matrix products  130 us (11%)
  blocking collectives  117 us (10%)
  other arithmetic  28.4 us (2%)
  between operations  15.4 us (1%)
    reduce_scatter x1, waiting for transfers between devices, body(): lax.psum_scatter(down_grad, 'dp', scatter_dimension=1, tiled=True)  100 us
    reduce_scatter x1, waiting for transfers between devices, body(): lax.psum_scatter(up_grad, 'dp', scatter_dimension=0, tiled=True)  99.7 us
    reduce_scatter x1, waiting for transfers between devices, body(): lax.psum_scatter(gate_grad, 'dp', scatter_dimension=0, tiled=True)  96.1 us
    reduce_scatter x1, waiting for transfers between devices, body(): lax.psum_scatter(in_grad_part, 'dp', scatter_dimension=0, tiled=True)  78 us
    reduce_scatter x1, waiting for transfers between devices, body(): lax.psum_scatter(out_grad_part, 'dp', scatter_dimension=1, tiled=True)  67.8 us
    reduce_scatter x1, waiting for transfers between devices, body(): lax.psum_scatter(jnp.dot(mixer_in, out_full, preferred_element_type=jnp.f...  50.9 us
    all_gather x1, waiting for transfers between devices, body(): lax.all_gather(gate_weight, 'dp', axis=0, tiled=True)  47.6 us
    reduce_scatter x1, waiting for transfers between devices, body(): lax.psum_scatter((jnp.einsum('tf,df->td', grad_gate, gate_again, preferre...  44.6 us
  transfers between devices with their start and end apart: 18, of which 16 were waited for; matrix products, arithmetic and copies ran while one was open for 8% of the time, Pallas kernels for 0%

commit v1 on v0

--- a/solution.py
+++ b/solution.py
@@ -1,12 +1,781 @@
+import functools
+
 import jax
 import jax.numpy as jnp
 from jax import lax
+from jax.experimental import pallas as pl
+from jax.experimental.pallas import tpu as pltpu
 from jax.sharding import PartitionSpec as P
 
 KW = 3
-
+MESH = pl.DeviceIdType.MESH
+BF = jnp.bfloat16
+F32 = jnp.float32
 
 epsilon = 1e-05
+
+NZ = 4
+CONV = 4
+FEED = 3
+Y_LAST = (True, False, True, False)
+
+
+def nn(a, b):
+    return lax.dot_general(a, b, (((1,), (0,)), ((), ())), preferred_element_type=F32)
+
+
+def nt(a, b):
+    return lax.dot_general(a, b, (((1,), (1,)), ((), ())), preferred_element_type=F32)
+
+
+def tn(a, b):
+    return lax.dot_general(a, b, (((0,), (0,)), ((), ())), preferred_element_type=F32)
+
+
+class Place:
+    def __init__(self):
+        self.dp = lax.axis_index("dp")
+        self.t = lax.axis_index("tensor")
+        self.z, self.x = lax.div(self.dp, 2), lax.rem(self.dp, 2)
+        self.y, self.c = lax.div(self.t, 2), lax.rem(self.t, 2)
+        self.over_x = (self.z * 2 + 1 - self.x, self.t)
+        self.over_y = (self.dp, (1 - self.y) * 2 + self.c)
+        self.over_c = (self.dp, self.y * 2 + 1 - self.c)
+        self.t_y = (1 - self.y) * 2 + self.c
+        self.t_c = self.y * 2 + 1 - self.c
+        self.t_yc = (1 - self.y) * 2 + 1 - self.c
+
+    def zs(self, k):
+        return lax.rem(self.z + k, NZ)
+
+    def over_z(self, k):
+        return (self.zs(k) * 2 + self.x, self.t)
+
+
+def greet(place, n_dp):
+    barrier = pltpu.get_barrier_semaphore()
+    for k in range(1, n_dp):
+        peer = (lax.rem(place.dp + k, n_dp), place.t)
+        pl.semaphore_signal(barrier, inc=1, device_id=peer, device_id_type=MESH)
+    for peer in (place.over_c, place.over_y):
+        pl.semaphore_signal(barrier, inc=1, device_id=peer, device_id_type=MESH)
+    pl.semaphore_wait(barrier, n_dp + 1)
+
+
+def remote(src, dst, send_sem, recv_sem, peer):
+    return pltpu.make_async_remote_copy(
+        src_ref=src, dst_ref=dst, send_sem=send_sem, recv_sem=recv_sem, device_id=peer, device_id_type=MESH
+    )
+
+
+def send(*what):
+    copy = remote(*what)
+    copy.start()
+    return copy
+
+
+def arrived(ref, sem, peer):
+    pltpu.make_async_remote_copy(
+        src_ref=ref, dst_ref=ref, send_sem=sem, recv_sem=sem, device_id=peer, device_id_type=MESH
+    ).wait_recv()
+
+
+def rows(start, size):
+    return pl.ds(pl.multiple_of(start, size), size)
+
+
+def forward_kernel(
+    n_dp,
+    tokens, cotangent, keep, small, in_own, out_own, gate_own, up_own, down_own,
+    conv_out, feed_out, normed_out, small_out, cot_out, proj_out, mixer_out, hidden_out, two_out, acts_out, down_out, down_y_out,
+    conv_w, feed_w, normed, small_all, mixed_pad, c_keep, proj, mixer_in, part_send, part_recv,
+    hidden, two, acts, down_send, down_recv,
+    own_sem, z_send, z_recv, x_send, x_recv, y_send, y_recv, fz_send, fz_recv, fx_send, fx_recv,
+    s_send, s_recv, a_send, a_recv, out_sem,
+):
+    place = Place()
+    z, x, y, c, t = place.z, place.x, place.y, place.c, place.t
+    depth = gate_own.shape[0]
+    local = tokens.shape[0]
+    chip = 2 * local
+    width = tokens.shape[1]
+    half = in_own.shape[2]
+    sends = []
+    copies = []
+    owned = {}
+
+    def conv_part(j, dp, n, side):
+        col = slice(None) if side is None else rows(side * half, half)
+        return conv_w.at[j, rows(dp * depth, n * depth), col]
+
+    def feed_part(w, dp):
+        return feed_w.at[w, rows(dp * depth, depth), :]
+
+    conv_own = [in_own.at[0], in_own.at[1], in_own.at[2], out_own]
+    feed_own = [gate_own, up_own, down_own]
+
+    greet(place, n_dp)
+
+    small_all[place.dp] = small[...]
+    for k in range(1, n_dp):
+        sends.append(send(small, small_all.at[place.dp], s_send.at[k], s_recv.at[place.dp],
+                          (lax.rem(place.dp + k, n_dp), t)))
+    own_copies = []
+    for j in range(CONV):
+        mine = conv_part(j, place.dp, 1, y)
+        for k in range(1, NZ):
+            sends.append(send(conv_own[j], mine, z_send.at[j, k], z_recv.at[j, z], place.over_z(k)))
+        if Y_LAST[j]:
+            sends.append(send(conv_own[j], mine, x_send.at[j, z], x_recv.at[j, z], place.over_x))
+        else:
+            sends.append(send(conv_own[j], mine, y_send.at[j, z], y_recv.at[j, z], place.over_y))
+        own = pltpu.make_async_copy(conv_own[j], mine, own_sem.at[j])
+        own.start()
+        own_copies.append(own)
+
+    def feed_start(w):
+        mine = feed_part(w, place.dp)
+        for k in range(1, NZ):
+            sends.append(send(feed_own[w], mine, fz_send.at[w, k], fz_recv.at[w, z], place.over_z(k)))
+        sends.append(send(feed_own[w], mine, fx_send.at[w, z], fx_recv.at[w, z], place.over_x))
+        owned[w] = pltpu.make_async_copy(feed_own[w], mine, own_sem.at[CONV + w])
+        owned[w].start()
+
+    def feed_forward_on(w, k):
+        zk = place.zs(k)
+        part = feed_part(w, zk * 2 + x)
+        arrived(part, fz_recv.at[w, zk], place.over_z(k))
+        sends.append(send(part, part, fx_send.at[w, zk], fx_recv.at[w, zk], place.over_x))
+
+    def feed_wait(w):
+        for k in range(NZ):
+            zk = place.zs(k)
+            arrived(feed_part(w, zk * 2 + 1 - x), fx_recv.at[w, zk], place.over_x)
+        owned[w].wait()
+        out(feed_w.at[w], feed_out.at[w], 7 + w)
+
+    def out(src, dst, index):
+        copy = pltpu.make_async_copy(src, dst, out_sem.at[index])
+        copy.start()
+        copies.append(copy)
+
+    feed_start(0)
+
+    cot_mine = cot_out.at[rows(t * local, local), :]
+    sends.append(send(cotangent, cot_mine, a_send.at[0], a_recv.at[0], place.over_c))
+    own_cot = pltpu.make_async_copy(cotangent, cot_mine, own_sem.at[CONV + FEED])
+    own_cot.start()
+
+    for k in range(1, n_dp):
+        peer = lax.rem(place.dp + k, n_dp)
+        arrived(small_all.at[peer], s_recv.at[peer], (peer, t))
+    gains = [jnp.concatenate([small_all[d, r : r + 1, :] for d in range(n_dp)], axis=1) for r in range(2)]
+    inputs = tokens[...].astype(F32)
+    inverse = lax.rsqrt(jnp.mean(inputs * inputs, axis=-1, keepdims=True) + epsilon)
+    normed[rows(c * local, local), :] = (inputs * inverse * gains[0]).astype(BF)
+    normed_mine = normed.at[rows(c * local, local), :]
+    sends.append(send(normed_mine, normed_mine, a_send.at[1], a_recv.at[1], place.over_c))
+
+    for k in range(1, NZ):
+        zk = place.zs(k)
+        for j in range(CONV):
+            part = conv_part(j, zk * 2 + x, 1, y)
+            arrived(part, z_recv.at[j, zk], place.over_z(k))
+            if Y_LAST[j]:
+                sends.append(send(part, part, x_send.at[j, zk], x_recv.at[j, zk], place.over_x))
+            else:
+                sends.append(send(part, part, y_send.at[j, zk], y_recv.at[j, zk], place.over_y))
+    for own in own_copies:
+        own.wait()
+    feed_start(1)
+    for k in range(NZ):
+        zk = place.zs(k)
+        for j in range(CONV):
+            if Y_LAST[j]:
+                arrived(conv_part(j, zk * 2 + 1 - x, 1, y), x_recv.at[j, zk], place.over_x)
+                pair = conv_part(j, zk * 2, 2, y)
+                sends.append(send(pair, pair, y_send.at[j, zk], y_recv.at[j, zk], place.over_y))
+            else:
+                arrived(conv_part(j, zk * 2 + x, 1, 1 - y), y_recv.at[j, zk], place.over_y)
+                pair = conv_part(j, zk * 2 + x, 1, None)
+                sends.append(send(pair, pair, x_send.at[j, zk], x_recv.at[j, zk], place.over_x))
+    sends.append(send(cotangent, cot_mine, a_send.at[2], a_recv.at[2], place.over_y))
+    for k in range(1, NZ):
+        feed_forward_on(0, k)
+    feed_start(2)
+    arrived(normed.at[rows((1 - c) * local, local), :], a_recv.at[1], place.over_c)
+    for j in range(CONV):
+        for k in range(NZ):
+            zk = place.zs(k)
+            if Y_LAST[j]:
+                arrived(conv_part(j, zk * 2, 2, 1 - y), y_recv.at[j, zk], place.over_y)
+            else:
+                arrived(conv_part(j, zk * 2 + 1 - x, 1, None), x_recv.at[j, zk], place.over_x)
+    out(conv_w, conv_out, 0)
+    out(normed, normed_out, 1)
+
+    tile = 256
+    pad = 8
+    mixed_pad[0:pad, :] = jnp.zeros((pad, 2 * half), F32)
+
+    def project(i, carry):
+        at = rows(i * tile, tile)
+        lhs = normed[at, :]
+        b = nn(lhs, conv_w[0])
+        proj[0, at, :] = b.astype(BF)
+        v = nn(lhs, conv_w[2])
+        proj[2, at, :] = v.astype(BF)
+        mixed_pad[pl.ds(pl.multiple_of(i * tile + pad, 8), tile), :] = b * v
+        g = nn(lhs, conv_w[1])
+        proj[1, at, :] = g.astype(BF)
+        c_keep[at, :] = g
+        return carry
+
+    lax.fori_loop(0, chip // tile, project, 0)
+
+    taps = []
+    for r in range(2, 2 + KW):
+        taps.append(jnp.concatenate(
+            [small_all[side * 4 + 2 * c + i, r : r + 1, :] for side in range(2) for i in range(2)], axis=1))
+
+    def convolve(i, carry):
+        at = rows(i * tile, tile)
+        window = mixed_pad[pl.ds(pl.multiple_of(i * tile, 8), tile + pad), :]
+        total = taps[0] * window[pad:, :]
+        for k in range(1, KW):
+            mask = jnp.concatenate([keep[k - 1, at, :]] * (2 * half // 128), axis=1)
+            total = total + mask * taps[k] * window[pad - k : pad - k + tile, :]
+        proj[3, at, :] = total.astype(BF)
+        mixer_in[at, :] = (c_keep[at, :] * total).astype(BF)
+        return carry
+
+    lax.fori_loop(0, chip // tile, convolve, 0)
+    out(proj, proj_out, 2)
+    out(mixer_in, mixer_out, 3)
+
+    part_send[...] = nt(mixer_in[rows((1 - c) * local, local), :], conv_w[3]).astype(BF)
+    sends.append(send(part_send, part_recv, a_send.at[3], a_recv.at[3], place.over_c))
+    hidden[...] = tokens[...].astype(F32) + nt(mixer_in[rows(c * local, local), :], conv_w[3])
+    arrived(part_recv, a_recv.at[3], place.over_c)
+    total = hidden[...] + part_recv[...].astype(F32)
+    hidden[...] = total
+    inverse = lax.rsqrt(jnp.mean(total * total, axis=-1, keepdims=True) + epsilon)
+    two[rows(t * local, local), :] = (total * inverse * gains[1]).astype(BF)
+    two_mine = two.at[rows(t * local, local), :]
+    sends.append(send(two_mine, two_mine, a_send.at[4], a_recv.at[4], place.over_c))
+    sends.append(send(two_mine, two_mine, a_send.at[5], a_recv.at[5], place.over_y))
+    hidden_copy = len(copies)
+    out(hidden, hidden_out, 4)
+
+    for k in range(1, NZ):
+        feed_forward_on(1, k)
+    there = cot_out.at[rows(place.t_y * local, local), :]
+    arrived(there, a_recv.at[2], place.over_y)
+    sends.append(send(there, there, a_send.at[6], a_recv.at[6], place.over_c))
+    feed_wait(0)
+    feed_wait(1)
+
+    def feed(block):
+        def step(i, carry):
+            at = rows(block * local + i * tile, tile)
+            lhs = two[at, :]
+            gate = nn(lhs, feed_w[0])
+            upward = nn(lhs, feed_w[1])
+            s = jax.nn.sigmoid(gate)
+            silu = gate * s
+            acts[0, at, :] = (silu * upward).astype(BF)
+            acts[1, at, :] = (upward * (s + silu * (1.0 - s))).astype(BF)
+            acts[2, at, :] = silu.astype(BF)
+            return carry
+
+        lax.fori_loop(0, local // tile, step, 0)
+
+    feed(t)
+    feed_forward_on(2, 1)
+    arrived(two.at[rows(place.t_c * local, local), :], a_recv.at[4], place.over_c)
+    there = two.at[rows(place.t_y * local, local), :]
+    arrived(there, a_recv.at[5], place.over_y)
+    sends.append(send(there, there, a_send.at[7], a_recv.at[7], place.over_c))
+    feed(place.t_c)
+    feed_forward_on(2, 2)
+    feed(place.t_y)
+    feed_forward_on(2, 3)
+    arrived(two.at[rows(place.t_yc * local, local), :], a_recv.at[7], place.over_c)
+    feed(place.t_yc)
+    out(acts, acts_out, 5)
+    out(two, two_out, 6)
+    small_out[...] = small_all[...]
+    feed_wait(2)
+    arrived(cot_out.at[rows(place.t_c * local, local), :], a_recv.at[0], place.over_c)
+    arrived(cot_out.at[rows(place.t_yc * local, local), :], a_recv.at[6], place.over_c)
+    own_cot.wait()
+
+    for i, block in enumerate((place.t_yc, place.t_c)):
+        down_send[i] = nt(acts[0, rows(block * local, local), :], feed_w[2]).astype(BF)
+        sends.append(send(down_send.at[i], down_recv.at[i], a_send.at[8 + i], a_recv.at[8 + i], place.over_c))
+    far = nt(acts[0, rows(place.t_y * local, local), :], feed_w[2])
+    arrived(down_recv.at[0], a_recv.at[8], place.over_c)
+    down_recv[0] = (far + down_recv[0].astype(F32)).astype(BF)
+    out(down_recv.at[0], down_y_out, 10)
+    copies[hidden_copy].wait()
+    hidden[...] = hidden[...] + nt(acts[0, rows(t * local, local), :], feed_w[2])
+    arrived(down_recv.at[1], a_recv.at[9], place.over_c)
+    hidden[...] = hidden[...] + down_recv[1].astype(F32)
+    out(hidden, down_out, 11)
+    for copy in sends:
+        copy.wait_send()
+    for i, copy in enumerate(copies):
+        if i != hidden_copy:
+            copy.wait()
+
+
+def forward_call(n_dp, *operands):
+    tokens, _, _, _, in_own, _, gate_own, _, _ = operands
+    local, width = tokens.shape
+    half, units = in_own.shape[2], gate_own.shape[1]
+    chip, group, mine = 2 * local, 4 * local, 2 * half
+
+    def shaped(dims, kind=BF):
+        return jax.ShapeDtypeStruct(dims, kind)
+
+    dma = pltpu.SemaphoreType.DMA
+    vmem, any_space = pl.BlockSpec(memory_space=pltpu.VMEM), pl.BlockSpec(memory_space=pl.ANY)
+    return pl.pallas_call(
+        functools.partial(forward_kernel, n_dp),
+        name="gather_forward",
+        out_shape=(
+            shaped((CONV, width, mine)), shaped((FEED, width, units)), shaped((chip, width)), shaped((n_dp, 8, 128), F32),
+            shaped((group, width)), shaped((4, chip, mine)), shaped((chip, mine)), shaped((local, width), F32),
+            shaped((group, width)), shaped((3, group, units)), shaped((local, width), F32), shaped((local, width)),
+        ),
+        in_specs=[vmem] * 4 + [any_space] * 5,
+        out_specs=tuple(vmem if i == 3 else any_space for i in range(12)),
+        scratch_shapes=[
+            pltpu.VMEM((CONV, width, mine), BF), pltpu.VMEM((FEED, width, units), BF), pltpu.VMEM((chip, width), BF),
+            pltpu.VMEM((n_dp, 8, 128), F32), pltpu.VMEM((chip + 8, mine), F32),
+            pltpu.VMEM((chip, mine), F32), pltpu.VMEM((4, chip, mine), BF), pltpu.VMEM((chip, mine), BF),
+            pltpu.VMEM((local, width), BF), pltpu.VMEM((local, width), BF), pltpu.VMEM((local, width), F32),
+            pltpu.VMEM((group, width), BF), pltpu.VMEM((3, group, units), BF),
+            pltpu.VMEM((2, local, width), BF), pltpu.VMEM((2, local, width), BF),
+            dma((8,)), dma((CONV, NZ)), dma((CONV, NZ)), dma((CONV, NZ)), dma((CONV, NZ)), dma((CONV, NZ)), dma((CONV, NZ)),
+            dma((FEED, NZ)), dma((FEED, NZ)), dma((FEED, NZ)), dma((FEED, NZ)),
+            dma((n_dp,)), dma((n_dp,)), dma((10,)), dma((10,)), dma((12,)),
+        ],
+        compiler_params=pltpu.CompilerParams(collective_id=0, has_side_effects=True, vmem_limit_bytes=62 << 20),
+    )(*operands)
+
+
+def backward_kernel(
+    n_dp,
+    tokens, cotangent, keep, small_all, conv_in, feed_in, normed_in, cot_in, proj_in, mixer_in_hbm, hidden_in, two_in, acts_in, down_in, down_y_in,
+    output, input_grad, in_grad, out_grad, gate_grad, up_grad, down_grad, small_grad,
+    act, g_down, x_got, z_got, g_conv, c_got_y, c_got_x, c_two, c_z, two_send, two_recv, two_y, own_two,
+    down_got, hidden, grad_mix, small_sum, small_got, small_z,
+    load_sem, fx_send, fx_recv, fz_send, fz_recv, c1_send, c1_recv, c2_send, c2_recv, c3_send, c3_recv,
+    s_send, s_recv, a_send, a_recv,
+):
+    place = Place()
+    z, x, y, c, t = place.z, place.x, place.y, place.c, place.t
+    depth = gate_grad.shape[0]
+    local, width = tokens.shape
+    chip = 2 * local
+    units = act.shape[1]
+    mine = g_conv.shape[2]
+    half = mine // 2
+    tile = 256
+    order = (1, 2, 3, 0)
+    sends = []
+
+    def post(make):
+        make().start()
+        sends.append(make)
+        return make
+
+    def load(src, dst, index):
+        copy = pltpu.make_async_copy(src, dst, load_sem.at[index])
+        copy.start()
+        return copy
+
+    greet(place, n_dp)
+    post(lambda: remote(down_y_in, down_got, a_send.at[0], a_recv.at[0], place.over_y))
+
+    def g_rows(w, start, size):
+        if w == 2:
+            return g_down.at[rows(start, size), :]
+        return act.at[rows(w * width + start, size), :]
+
+    def feed_x(w, k):
+        def make():
+            zk = place.zs(k)
+            return remote(g_rows(w, (zk * 2 + 1 - x) * depth, depth), x_got.at[w, zk], fx_send.at[w, zk], fx_recv.at[w, zk], place.over_x)
+
+        post(make)
+
+    def feed_z(w, k):
+        zk = place.zs(k)
+        got = x_got.at[w, zk]
+        arrived(got, fx_recv.at[w, zk], place.over_x)
+        if k:
+            got[...] = (g_rows(w, (zk * 2 + x) * depth, depth)[...].astype(F32) + got[...].astype(F32)).astype(BF)
+            post(lambda: remote(x_got.at[w, place.zs(k)], z_got.at[w, NZ - k - 1], fz_send.at[w, k], fz_recv.at[w, NZ - k], place.over_z(k)))
+
+    def feed_end(w):
+        total = g_rows(w, (z * 2 + x) * depth, depth)[...].astype(F32) + x_got[w, z].astype(F32)
+        for k in range(1, NZ):
+            arrived(z_got.at[w, k - 1], fz_recv.at[w, k], place.over_z(k))
+            total = total + z_got[w, k - 1].astype(F32)
+        return total
+
+    def first_slot():
+        return remote(two_send.at[0], two_recv.at[0], a_send.at[1], a_recv.at[1], place.over_c)
+
+    def feed_phase(feed_w, cot, acts):
+        loads = [load(acts_in.at[0], act, 0), load(cot_in, cot, 1), load(feed_in, feed_w, 2),
+                 load(acts_in.at[1], acts.at[0], 3), load(acts_in.at[2], acts.at[1], 4), load(hidden_in, hidden, 5)]
+        loads[0].wait()
+        loads[1].wait()
+        for k in order:
+            at = rows(place.zs(k) * 2 * depth, 2 * depth)
+            g_down[at, :] = tn(cot[:, at], act[...]).astype(BF)
+            feed_x(2, k)
+        for index in (2, 3, 4):
+            loads[index].wait()
+
+        def back(block, store):
+            def step(i, carry):
+                at = rows(block * local + i * tile, tile)
+                grad_act = nn(cot[at, :], feed_w[2])
+                grad_gate = (grad_act * acts[0, at, :].astype(F32)).astype(BF)
+                acts[0, at, :] = grad_gate
+                grad_up = (grad_act * acts[1, at, :].astype(F32)).astype(BF)
+                acts[1, at, :] = grad_up
+                store(rows(i * tile, tile), nt(grad_gate, feed_w[0]) + nt(grad_up, feed_w[1]))
+                return carry
+
+            lax.fori_loop(0, local // tile, step, 0)
+
+        def to_slot(slot):
+            def store(at, value):
+                two_send[slot, at, :] = value.astype(BF)
+
+            return store
+
+        def to_own(at, value):
+            own_two[at, :] = value
+
+        back(place.t_yc, to_slot(0))
+        post(first_slot)
+        feed_z(2, 1)
+        back(place.t_y, to_own)
+        arrived(two_recv.at[0], a_recv.at[1], place.over_c)
+        two_recv[0] = (own_two[...] + two_recv[0].astype(F32)).astype(BF)
+        post(lambda: remote(two_recv.at[0], two_y, a_send.at[2], a_recv.at[2], place.over_y))
+        feed_z(2, 2)
+        back(place.t_c, to_slot(1))
+        post(lambda: remote(two_send.at[1], two_recv.at[1], a_send.at[3], a_recv.at[3], place.over_c))
+        feed_z(2, 3)
+        feed_z(2, 0)
+        back(t, to_own)
+        two = load(two_in, cot, 6)
+        two.wait()
+        for w in (0, 1):
+            for k in order:
+                at = rows(place.zs(k) * 2 * depth, 2 * depth)
+                act[rows(w * width + place.zs(k) * 2 * depth, 2 * depth), :] = tn(cot[:, at], acts[w]).astype(BF)
+                feed_x(w, k)
+                if w == 1:
+                    feed_z(0, k)
+        loads[5].wait()
+
+    pl.run_scoped(
+        feed_phase,
+        pltpu.VMEM((FEED, width, units), BF), pltpu.VMEM((4 * local, width), BF), pltpu.VMEM((2, 4 * local, units), BF),
+    )
+
+    gains = [jnp.concatenate([small_all[d, r : r + 1, :] for d in range(n_dp)], axis=1) for r in range(2)]
+
+    def norm_back(grad, unit, inverse, gain):
+        scaled = grad * gain
+        return inverse * (scaled - unit * jnp.mean(scaled * unit, axis=-1, keepdims=True))
+
+    def rms(values):
+        return lax.rsqrt(jnp.mean(values * values, axis=-1, keepdims=True) + epsilon)
+
+    def c1_slot(j, zk):
+        return c_got_y.at[j // 2, zk] if Y_LAST[j] else c_got_x.at[j // 2, zk]
+
+    def conv_first(j, k):
+        def make():
+            zk = place.zs(k)
+            if Y_LAST[j]:
+                src, peer = g_conv.at[j, rows(zk * 2 * depth, 2 * depth), rows((1 - y) * half, half)], place.over_y
+            else:
+                src, peer = g_conv.at[j, rows((zk * 2 + 1 - x) * depth, depth), :], place.over_x
+            return remote(src, c1_slot(j, zk), c1_send.at[j, zk], c1_recv.at[j, zk], peer)
+
+        post(make)
+
+    def conv_second(j, k):
+        zk = place.zs(k)
+        got = c1_slot(j, zk)
+        if Y_LAST[j]:
+            arrived(got, c1_recv.at[j, zk], place.over_y)
+            held = g_conv[j, rows(zk * 2 * depth, 2 * depth), rows(y * half, half)]
+        else:
+            arrived(got, c1_recv.at[j, zk], place.over_x)
+            held = g_conv[j, rows((zk * 2 + x) * depth, depth), :]
+        got[...] = (held.astype(F32) + got[...].astype(F32)).astype(BF)
+
+        def make():
+            zk = place.zs(k)
+            if Y_LAST[j]:
+                src, peer = c1_slot(j, zk).at[rows((1 - x) * depth, depth), :], place.over_x
+            else:
+                src, peer = c1_slot(j, zk).at[:, rows((1 - y) * half, half)], place.over_y
+            return remote(src, c_two.at[j, zk], c2_send.at[j, zk], c2_recv.at[j, zk], peer)
+
+        post(make)
+
+    def conv_third(j, k):
+        zk = place.zs(k)
+        if Y_LAST[j]:
+            arrived(c_two.at[j, zk], c2_recv.at[j, zk], place.over_x)
+            held = c_got_y[j // 2, zk, rows(x * depth, depth), :]
+        else:
+            arrived(c_two.at[j, zk], c2_recv.at[j, zk], place.over_y)
+            held = c_got_x[j // 2, zk, :, rows(y * half, half)]
+        if k:
+            c_two[j, zk] = (held.astype(F32) + c_two[j, zk].astype(F32)).astype(BF)
+            post(lambda: remote(c_two.at[j, place.zs(k)], c_z.at[j, NZ - k - 1], c3_send.at[j, k], c3_recv.at[j, NZ - k], place.over_z(k)))
+
+    def conv_end(j):
+        if Y_LAST[j]:
+            held = c_got_y[j // 2, z, rows(x * depth, depth), :]
+        else:
+            held = c_got_x[j // 2, z, :, rows(y * half, half)]
+        total = held.astype(F32) + c_two[j, z].astype(F32)
+        for k in range(1, NZ):
+            arrived(c_z.at[j, k - 1], c3_recv.at[j, k], place.over_z(k))
+            total = total + c_z[j, k - 1].astype(F32)
+        return total
+
+    def conv_phase(conv_w, proj, normed, mixer_in, grad_proj, pad_grad, tap_sum):
+        loads = [load(conv_in, conv_w, 0), load(mixer_in_hbm, mixer_in, 1), load(proj_in, proj, 2), load(normed_in, normed, 3)]
+
+        arrived(two_y, a_recv.at[2], place.over_y)
+        arrived(two_recv.at[1], a_recv.at[3], place.over_c)
+
+        def second_norm(i, carry):
+            at = rows(i * 128, 128)
+            grad_two = own_two[at, :] + two_recv[1, at, :].astype(F32) + two_y[at, :].astype(F32)
+            values = hidden[at, :]
+            inverse = rms(values)
+            unit = values * inverse
+            grad_hidden = cotangent[at, :].astype(F32) + norm_back(grad_two, unit, inverse, gains[1])
+            hidden[at, :] = grad_hidden
+            grad_mix[rows(c * local + i * 128, 128), :] = grad_hidden.astype(BF)
+            return carry + jnp.sum(grad_two * unit, axis=0, keepdims=True)
+
+        feed_gain = lax.fori_loop(0, local // 128, second_norm, jnp.zeros((1, width), F32))
+
+        def send_mix():
+            mix_mine = grad_mix.at[rows(c * local, local), :]
+            return remote(mix_mine, mix_mine, a_send.at[4], a_recv.at[4], place.over_c)
+
+        post(send_mix)
+        for k in order:
+            feed_z(1, k)
+        for copy in loads:
+            copy.wait()
+        arrived(grad_mix.at[rows((1 - c) * local, local), :], a_recv.at[4], place.over_c)
+
+        taps = []
+        for r in range(2, 2 + KW):
+            taps.append(jnp.concatenate(
+                [small_all[side * 4 + 2 * c + i, r : r + 1, :] for side in range(2) for i in range(2)], axis=1))
+        pad_grad[pl.ds(chip, 8), :] = jnp.zeros((8, mine), F32)
+
+        def first_half(i, carry):
+            at = rows(i * tile, tile)
+            grad_in = nn(grad_mix[at, :], conv_w[3])
+            grad_proj[1, at, :] = (grad_in * proj[3, at, :].astype(F32)).astype(BF)
+            pad_grad[at, :] = grad_in * proj[1, at, :].astype(F32)
+            return carry
+
+        lax.fori_loop(0, chip // tile, first_half, 0)
+
+        def weight_grad(j, lhs, rhs):
+            g_conv[j] = tn(lhs, rhs).astype(BF)
+            for k in order:
+                conv_first(j, k)
+
+        weight_grad(3, grad_mix[...], mixer_in[...])
+        weight_grad(1, normed[...], grad_proj[1])
+        tap_sum[...] = jnp.zeros_like(tap_sum)
+        small_tile = 128
+
+        def second_half(i, carry):
+            at = rows(i * small_tile, small_tile)
+            wide = pl.ds(pl.multiple_of(i * small_tile, 8), small_tile + 8)
+            window = pad_grad[wide, :]
+            b, v = proj[0, at, :].astype(F32), proj[2, at, :].astype(F32)
+            mixed = b * v
+            now = window[:small_tile, :]
+            total = taps[0] * now
+            tap_sum[0:1, :] += jnp.sum(now * mixed, axis=0, keepdims=True)
+            for k in range(1, KW):
+                mask = jnp.concatenate([keep[k - 1, wide, :]] * (mine // 128), axis=1)
+                ahead = (mask * window)[k : k + small_tile, :]
+                total = total + taps[k] * ahead
+                tap_sum[k : k + 1, :] += jnp.sum(ahead * mixed, axis=0, keepdims=True)
+            grad_proj[0, at, :] = (total * v).astype(BF)
+            grad_proj[2, at, :] = (total * b).astype(BF)
+            return carry
+
+        lax.fori_loop(0, chip // small_tile, second_half, 0)
+        weight_grad(0, normed[...], grad_proj[0])
+        weight_grad(2, normed[...], grad_proj[2])
+
+        def first_grad(block):
+            at = rows(block * local, local)
+            return nt(grad_proj[0, at, :], conv_w[0]) + nt(grad_proj[1, at, :], conv_w[1]) + nt(grad_proj[2, at, :], conv_w[2])
+
+        first_slot().wait_send()
+        sends.remove(first_slot)
+        two_send[0] = first_grad(1 - c).astype(BF)
+        post(lambda: remote(two_send.at[0], two_recv.at[1], a_send.at[5], a_recv.at[5], place.over_c))
+        own_two[...] = first_grad(c)
+        for k in order:
+            for j in (3, 1):
+                conv_second(j, k)
+        arrived(two_recv.at[1], a_recv.at[5], place.over_c)
+
+        def first_norm(i, carry):
+            at = rows(i * 128, 128)
+            grad_one = own_two[at, :] + two_recv[1, at, :].astype(F32)
+            values = tokens[at, :].astype(F32)
+            inverse = rms(values)
+            unit = values * inverse
+            two_recv[1, at, :] = (hidden[at, :] + norm_back(grad_one, unit, inverse, gains[0])).astype(BF)
+            return carry + jnp.sum(grad_one * unit, axis=0, keepdims=True)
+
+        mixer_gain = lax.fori_loop(0, local // 128, first_norm, jnp.zeros((1, width), F32))
+        zero = jnp.zeros((1, 128), F32)
+        for d in range(n_dp):
+            cols = slice(d * 128, d * 128 + 128)
+            here = (c == (d % 4) // 2).astype(F32)
+            own = (d // 4) * half + (d % 2) * 128
+            small_sum[d] = jnp.concatenate(
+                [mixer_gain[:, cols], feed_gain[:, cols]]
+                + [here * tap_sum[k : k + 1, own : own + 128] for k in range(KW)] + [zero] * 3, axis=0)
+
+    pl.run_scoped(
+        conv_phase,
+        pltpu.VMEM((CONV, width, mine), BF), pltpu.VMEM((4, chip, mine), BF), pltpu.VMEM((chip, width), BF),
+        pltpu.VMEM((chip, mine), BF), pltpu.VMEM((3, chip, mine), BF), pltpu.VMEM((chip + 8, mine), F32), pltpu.VMEM((8, mine), F32),
+    )
+
+    input_copy = load(two_recv.at[1], input_grad, 5)
+    post(lambda: remote(small_sum, small_got.at[0], s_send.at[0], s_recv.at[0], place.over_c))
+    for k in order:
+        for j in (0, 2):
+            conv_second(j, k)
+    arrived(small_got.at[0], s_recv.at[0], place.over_c)
+    small_got[0] = small_sum[...] + small_got[0]
+    post(lambda: remote(small_got.at[0], small_got.at[1], s_send.at[1], s_recv.at[1], place.over_y))
+    for k in order:
+        for j in (3, 1):
+            conv_third(j, k)
+    final = load(down_in, own_two, 4)
+    for w, ref in ((2, None), (0, gate_grad), (1, up_grad)):
+        total = feed_end(w)
+        if ref is None:
+            down_grad[...] = jnp.transpose(total)
+        else:
+            ref[...] = total
+    arrived(small_got.at[1], s_recv.at[1], place.over_y)
+    small_got[1] = small_got[0] + small_got[1]
+    for k in range(NZ):
+        zk = place.zs(k)
+        post(lambda zk=zk, k=k: remote(small_got.at[1, zk * 2 + 1 - x], small_z.at[zk], s_send.at[2 + k], s_recv.at[2 + zk], place.over_x))
+    for k in order:
+        for j in (0, 2):
+            conv_third(j, k)
+    arrived(down_got, a_recv.at[0], place.over_y)
+    final.wait()
+    down_got[...] = (own_two[...] + down_got[...].astype(F32)).astype(BF)
+    output_copy = load(down_got, output, 6)
+    for k in order:
+        zk = place.zs(k)
+        arrived(small_z.at[zk], s_recv.at[2 + zk], place.over_x)
+        small_z[zk] = small_z[zk] + small_got[1, zk * 2 + x]
+        if k:
+            post(lambda zk=zk, k=k: remote(
+                small_z.at[zk], small_z.at[NZ + NZ - k], s_send.at[6 + k], s_recv.at[6 + NZ - k], place.over_z(k)))
+    out_grad[...] = jnp.transpose(conv_end(3))
+    in_grad[1] = conv_end(1)
+    in_grad[0] = conv_end(0)
+    in_grad[2] = conv_end(2)
+    total = small_z[z]
+    for k in range(1, NZ):
+        arrived(small_z.at[NZ + k], s_recv.at[6 + k], place.over_z(k))
+        total = total + small_z[NZ + k]
+    small_grad[...] = total
+    for make in sends:
+        make().wait_send()
+    input_copy.wait()
+    output_copy.wait()
+
+
+def backward_call(n_dp, tokens, cotangent, keep, small_all, conv_w, feed_w, *rest):
+    local, width = tokens.shape
+    units, mine = feed_w.shape[2], conv_w.shape[2]
+    chip, half, depth = 2 * local, mine // 2, width // n_dp
+
+    def shaped(dims, kind=BF):
+        return jax.ShapeDtypeStruct(dims, kind)
+
+    dma = pltpu.SemaphoreType.DMA
+    vmem, any_space = pl.BlockSpec(memory_space=pltpu.VMEM), pl.BlockSpec(memory_space=pl.ANY)
+    return pl.pallas_call(
+        functools.partial(backward_kernel, n_dp),
+        name="backward_scatter",
+        out_shape=(
+            shaped((local, width)), shaped((local, width)), shaped((3, depth, half), F32), shaped((half, depth), F32),
+            shaped((depth, units), F32), shaped((depth, units), F32), shaped((units, depth), F32), shaped((8, 128), F32),
+        ),
+        in_specs=[vmem] * 4 + [any_space] * (2 + len(rest)),
+        out_specs=(any_space,) * 2 + (vmem,) * 6,
+        scratch_shapes=[
+            pltpu.VMEM((4 * local, units), BF), pltpu.VMEM((width, units), BF), pltpu.VMEM((FEED, NZ, depth, units), BF),
+            pltpu.VMEM((FEED, NZ - 1, depth, units), BF), pltpu.VMEM((CONV, width, mine), BF),
+            pltpu.VMEM((2, NZ, 2 * depth, half), BF), pltpu.VMEM((2, NZ, depth, mine), BF), pltpu.VMEM((CONV, NZ, depth, half), BF),
+            pltpu.VMEM((CONV, NZ - 1, depth, half), BF), pltpu.VMEM((2, local, width), BF), pltpu.VMEM((2, local, width), BF),
+            pltpu.VMEM((local, width), BF), pltpu.VMEM((local, width), F32), pltpu.VMEM((local, width), BF),
+            pltpu.VMEM((local, width), F32), pltpu.VMEM((chip, width), BF), pltpu.VMEM((n_dp, 8, 128), F32),
+            pltpu.VMEM((2, n_dp, 8, 128), F32), pltpu.VMEM((2 * NZ, 8, 128), F32),
+            dma((7,)), dma((FEED, NZ)), dma((FEED, NZ)), dma((FEED, NZ)), dma((FEED, NZ)), dma((CONV, NZ)), dma((CONV, NZ)),
+            dma((CONV, NZ)), dma((CONV, NZ)), dma((CONV, NZ)), dma((CONV, NZ)), dma((10,)), dma((10,)), dma((6,)), dma((6,)),
+        ],
+        compiler_params=pltpu.CompilerParams(collective_id=1, has_side_effects=True, vmem_limit_bytes=63 << 20),
+    )(tokens, cotangent, keep, small_all, conv_w, feed_w, *rest)
+
+
+def block(n_dp, tokens, doc_ids, mixer_norm, in_weight, conv_weight, out_weight, feed_norm, gate_weight, up_weight, down_weight, out_grad):
+    chip = 2 * tokens.shape[0]
+    documents = lax.dynamic_index_in_dim(doc_ids, lax.div(lax.axis_index("tensor"), 2), 0, keepdims=False)
+    keep = []
+    for offset in range(1, KW):
+        same = jnp.concatenate([jnp.zeros((offset,), bool), documents[offset:] == documents[:-offset], jnp.zeros((8,), bool)])
+        keep.append(jnp.broadcast_to(same.astype(F32)[:, None], (chip + 8, 128)))
+    keep = jnp.stack(keep)
+    small = jnp.concatenate(
+        [mixer_norm[None], feed_norm[None], conv_weight, jnp.zeros((6 - KW, mixer_norm.shape[0]), BF)], axis=0).astype(F32)
+    conv_w, feed_w, normed, small_all, cot, proj, mixer_in, hidden, two, acts, down, down_y = forward_call(
+        n_dp, tokens, out_grad, keep, small, in_weight.transpose(1, 0, 2), out_weight.T, gate_weight, up_weight, down_weight.T)
+    output, input_grad, in_g, out_g, gate_g, up_g, down_g, small_g = backward_call(
+        n_dp, tokens, out_grad, keep, small_all, conv_w, feed_w, normed, cot, proj, mixer_in, hidden, two, acts, down, down_y)
+    return (output, input_grad, small_g[0], in_g.transpose(1, 0, 2), small_g[2 : 2 + KW], out_g, small_g[1], gate_g, up_g, down_g)
 
 
 def shift_down(values, offset):
@@ -249,4 +1018,7 @@
         P("dp", "tensor"),
         P("tensor", "dp"),
     )
-    return jax.shard_map(body, mesh=mesh, in_specs=in_specs, out_specs=out_specs, check_vma=False)
+    n_dp = mesh.shape["dp"]
+    fits = n_dp == 2 * NZ and mesh.shape["tensor"] == 4
+    step = functools.partial(block, n_dp) if fits else body
+    return jax.shard_map(step, mesh=mesh, in_specs=in_specs, out_specs=out_specs, check_vma=False)

time: 1160 us -> 349 us (0.30)
  waiting for transfers between devices: 856 us -> 0 us
  Pallas kernels: 0 us -> 327 us
  matrix products: 130 us -> 0 us
  blocking collectives: 117 us -> 0 us
  other arithmetic: 28.4 us -> 4.13 us
  between operations: 15.4 us -> 0.95 us
    reduce_scatter x9 -> x0, waiting for transfers between devices: 597 us -> none  [the longest x1 100 us: body(): lax.psum_scatter(down_grad, 'dp', scatter_dimension=1, tiled=True)]
    pallas_call x0 -> x2, Pallas kernels: none -> 327 us  [the longest x1 173 us: backward_call(): pl.pallas_call(functools.partial(backward_kernel, n_dp), name='backward_s...]
    all_gather x8 -> x0, waiting for transfers between devices: 255 us -> none  [the longest x1 47.6 us: body(): lax.all_gather(gate_weight, 'dp', axis=0, tiled=True)]
    dot_general x15 -> x0, matrix products: 130 us -> none  [the longest x1 18 us: body(): jnp.einsum('td,fd->tf', cotangent, down_again, preferred_element_type=jnp...]
    all_gather x4 -> x0, blocking collectives: 89.1 us -> none  [the longest x1 30.1 us: body(): lax.all_gather(out_weight, 'dp', axis=1, tiled=True)]
    unnamed x1 -> x0, blocking collectives: 21.6 us -> none
  transfers between devices with their start and end apart: 18 -> 0, of which waited for: 16 -> 0; matrix products, arithmetic and copies ran while one was open for 8% -> 0% of each run, Pallas kernels for 0% -> 0%
where the time goes in v1:
time: 349 us; the launch traced here: 346 us
  Pallas kernels  327 us (94%)
  local copies, waits for them, and re-layouts  13.8 us (4%)
  other arithmetic  4.13 us (1%)
    pallas_call x1, Pallas kernels, backward_call(): pl.pallas_call(functools.partial(backward_kernel, n_dp), name='backward_s...  173 us
    pallas_call x1, Pallas kernels, forward_call(): pl.pallas_call(functools.partial(forward_kernel, n_dp), name='gather_forw...  155 us
    unnamed x21, local copies, waits for them, and re-layouts  10.6 us

profile of v1, /device:TPU:0, one launch (start us, length us, event | category | flops | bytes accessed | tf_op | source)
XLA Modules:
  0.0 346.1 jit_solution(11811089018831507050)
XLA Ops:
  0.7 0.9 compare_reduce_fusion.1
  1.5 0.9 compare_reduce_fusion
  2.4 0.1 concatenate.10
  2.5 0.1 concatenate.9
  2.6 0.1 pad.3.clone
  2.7 1.4 maximum_convert_fusion.small
  4.0 1.6 copy.21
  5.6 1.8 copy.22
  7.5 0.2 stack_broadcast_in_dim.5
  7.7 0.2 stack_broadcast_in_dim.4
  7.9 1.0 pad_maximum_fusion.keep
  8.9 154.7 %gather_forward.1 = (bf16[4,1024,512]{2,1,0:T(8,128)(2,1)}, bf16[3,1024,1152]{2,1,0:T(8,128)(2,1)}, bf16[1024,1024]{1,0:T(8,128)(2,1)}, f32[8,8,128]{2,1,0:T(8,1...) custom-call(bf16[512,1024]{1,0:T(8,128)(2,1)} %tokens.3, ...), custom_call_target="tpu_custom_call" | custom-call | tf_op jit(solution)/shard_map/gather_forward/pallas_call | solution.py:343
  163.6 172.6 %backward_scatter.1 = (bf16[512,1024]{1,0:T(8,128)(2,1)}, bf16[512,1024]{1,0:T(8,128)(2,1)}, f32[3,128,256]{2,1,0:T(8,128)}, f32[256,128]{1,0:T(8,128)}, f32[128...) custom-call(bf16[512,1024]{1,0:T(8,128)(2,1)} %tokens.3, ...), custom_call_target="tpu_custom_call" | custom-call | tf_op jit(solution)/shard_map/backward_scatter/pallas_call | solution.py:740
  336.1 0.0 copy-start
  336.1 1.3 slice_bitcast_fusion
  337.4 1.3 slice.30
  338.7 2.3 copy.30
  341.0 1.0 copy.31
  342.0 0.0 copy-done.4
  342.0 0.7 copy.32
  342.7 0.7 copy.33
  343.4 0.8 copy.34
  344.2 0.8 copy.35
  345.0 0.8 copy.36
  (15 shorter events, 0.0 us)
Async XLA Ops:
  336.1 4.9 %copy-start = (bf16[512,1024]{1,0:T(8,128)(2,1)S(1)}, bf16[512,1024]{1,0:T(8,128)(2,1)}, u32[]{:S(2)}) copy-start(bf16[512,1024]{1,0:T(8,128)(2,1)} %get-tuple-element.63) | copy-start | bytes 3145732
  338.7 3.3 copy-start.4
  338.7 4.1 %copy-start.5 = (f32[256,128]{1,0:T(8,128)S(1)}, f32[256,128]{1,0:T(8,128)}, u32[]{:S(2)}) copy-start(f32[256,128]{1,0:T(8,128)} %get-tuple-element.67) | copy-start | bytes 393220
  341.0 2.4 copy-start.3
  341.0 3.2 copy-start.2
  342.0 3.0 copy-start.1
